TPU v7x, 512 devices: a whole 4x8x8 slice. The times are simulated.
512 devices in a mesh: lat: 64 (over z, x, core), rad: 8 (over y).
Axes of the slice: x: 4, y: 8, z: 8, core: 2. Of those that a mesh axis runs over, the one named last changes fastest.
Arguments:
- fourier: bfloat16 [2, 2, 256, 2, 64, 1152], P(None, None, 'rad', None, None, 'lat'), may hold values from -6 to 6
- legendre: bfloat16 [64, 1024, 1152], P('lat'), may hold values from -0.1875 to 0.1875
- inverse: bfloat16 [1024, 512, 512], P('lat', 'rad'), may hold values from -0.25 to 0.25
- order_of_slot: int32 [64], replicated, may hold values from 0 to 63, each once
- degree_of_slot: int32 [1024], replicated, may hold values from 0 to 1023, each once
- degree_count: int32 [64], replicated, may hold values from 1 to 1024, as said below
Outputs:
- solved: float32 [1024, 512, 2, 64], P('lat', 'rad')
Inputs may be any that keep to these rules, and one draw needn't show every extreme that they name: `order_of_slot`: a permutation; the index p of lat is given slot p. `degree_of_slot`: a permutation; the index p of lat is given slots p * 16 to (p + 1) * 16 - 1. Order k is live on the last degree_count[k] degrees of the band; some order has all 1024.
All inputs are finite; a program needn't handle non-finite values.
Results may differ from a plain program's by a relative error of at most 0.0042.
Values may be sent and summed in bfloat16 or wider, within the bound.
A program may use at most 64 MiB of HBM per device.

v0:
```python
import jax
import jax.numpy as jnp
from jax import lax
from jax.sharding import PartitionSpec as P


def analyze(received, legendre, first_live):
    north_rows = received[:, :, :, 0].astype(jnp.float32)
    south_rows = received[:, :, :, 1].astype(jnp.float32)
    even_part = (north_rows + south_rows).astype(jnp.bfloat16)
    odd_part = (north_rows - south_rows).astype(jnp.bfloat16)
    slot_count = legendre.shape[0]
    band_size = legendre.shape[1]
    band_index = lax.broadcasted_iota(jnp.int32, (slot_count, band_size), 1)
    live_mask = band_index >= first_live[:, None]
    use_even = (band_index - first_live[:, None]) % 2 == 0
    full_even = jnp.einsum(
        "ojn,fcron->ojfcr", legendre, even_part, preferred_element_type=jnp.float32
    )
    full_odd = jnp.einsum(
        "ojn,fcron->ojfcr", legendre, odd_part, preferred_element_type=jnp.float32
    )
    chosen = jnp.where(use_even[:, :, None, None, None], full_even, full_odd)
    return jnp.where(live_mask[:, :, None, None, None], chosen, 0.0).astype(jnp.bfloat16)


def on_device(fourier, legendre, inverse, order_of_slot, degree_of_slot, degree_count):
    slot_count = legendre.shape[0]
    band_size = legendre.shape[1]
    lat_index = lax.axis_index("lat")
    my_orders = lax.dynamic_slice_in_dim(order_of_slot, lat_index * slot_count, slot_count)
    first_live = band_size - jnp.take(degree_count, my_orders)
    picked = jnp.take(fourier, order_of_slot, axis=4)
    received = lax.all_to_all(picked, "lat", split_axis=4, concat_axis=5, tiled=True)
    coefficients = analyze(received, legendre, first_live)
    by_degree = jnp.take(coefficients, degree_of_slot, axis=1)
    at_owner = lax.all_to_all(by_degree, "lat", split_axis=1, concat_axis=0, tiled=True)
    degree_local = inverse.shape[0]
    row_block = inverse.shape[1]
    full_rows = inverse.shape[2]
    matrices = inverse.reshape(degree_local, row_block, 2, full_rows // 2)
    return jnp.einsum(
        "tqfk,mtfck->tqcm",
        matrices,
        lax.all_gather(at_owner, "rad", axis=4, tiled=True),
        preferred_element_type=jnp.float32,
    )


def solution(mesh):
    in_specs = (
        P(None, None, "rad", None, None, "lat"),
        P("lat", None, None),
        P("lat", "rad", None),
        P(),
        P(),
        P(),
    )
    out_specs = P("lat", "rad", None, None)
    return jax.shard_map(
        on_device, mesh=mesh, in_specs=in_specs, out_specs=out_specs, check_vma=False
    )
```

profile of v0, /device:TPU:1, one launch (start us, length us, event | category | flops | bytes accessed | tf_op | source)
XLA Modules:
  0.0 196.2 jit_solution(13776918970840271404)
XLA Ops:
  6.5 0.0 copy-start
  6.5 0.8 compare_select_fusion.1
  7.3 0.7 compare_and_fusion.1
  8.0 7.4 %copy.17 = bf16[2,2,32,2,64,18]{2,5,3,1,0,4:T(8,128)(2,1)} copy(bf16[2,2,32,2,64,18]{4,3,5,2,1,0:T(2,128)(2,1)} %param.6) | data formatting | bytes 1179648 | tf_op args[0]
  15.4 4.5 %gather_fusion = bf16[64,2,2,32,2,18]{3,5,4,2,1,0:T(8,128)(2,1)} fusion(bf16[2,2,32,2,64,18]{2,5,3,1,0,4:T(8,128)(2,1)} %copy.17, s32[1024]{0:T(1024)S(1)} %pad_clamp_fusion), kind=kCustom, calls=%fused_computation | custom fusion | bytes 1179904 | tf_op jit(solution)/shard_map/jit(_take)/gather | solution.py:33
  19.9 2.2 %select_bitcast_fusion = bf16[2,2,32,2,64,18]{2,5,3,1,0,4:T(8,128)(2,1)S(1)} fusion(bf16[64,2,2,32,2,18]{3,5,4,2,1,0:T(8,128)(2,1)} %gather_fusion, pred[64]{0:T(512)(128)(4,1)S(1)} %compare_and_fusion.1), kind=kLoop, calls=%fused_computation.2 | loop fusion | flops 294912 | bytes 1179712 | tf_op jit(solution)/shard_map/jit(_take)/select_n | solution.py:33
  22.2 3.8 %copy.36 = bf16[2,2,32,2,64,18]{2,3,5,1,0,4:T(2,128)(2,1)} copy(bf16[2,2,32,2,64,18]{2,5,3,1,0,4:T(8,128)(2,1)S(1)} %select_bitcast_fusion) | data formatting | bytes 1179648 | tf_op jit(solution)/shard_map/jit(_take)/select_n | solution.py:33
  26.0 6.4 %reshape.148 = bf16[64,2,2304]{2,1,0:T(2,128)(2,1)} reshape(bf16[64,2,2,18,2,32]{5,4,3,2,1,0:T(2,128)(2,1)} %bitcast.59) | data formatting | bytes 1179648
  32.4 14.8 %all-to-all-start = ((bf16[64,2,2304]{2,1,0:T(2,128)(2,1)}), bf16[64,2,2304]{2,1,0:T(2,128)(2,1)S(1)}, u32[]{:S(2)}, u32[]{:S(2)}) async-start(bf16[64,2,2304]{2,1,0:T(2,128)(2,1)} %reshape.148), calls=%async_computation | async-start | bytes 1179648 | tf_op jit(solution)/shard_map/all_to_all | solution.py:34
  47.3 0.2 all-gather.2.cloned.1.call-start
  47.5 0.0 copy-done.2
  47.5 0.6 dynamic_slice.3
  50.0 0.0 copy-done.3
  50.0 0.6 dynamic-slice.2
  51.4 14.9 %all-to-all-done = bf16[64,2,2304]{2,1,0:T(2,128)(2,1)S(1)} async-done(((bf16[64,2,2304]{2,1,0:T(2,128)(2,1)}), bf16[64,2,2304]{2,1,0:T(2,128)(2,1)S(1)}, u32[]{:S(2)}, u32[]{:S(2)}) %all-to-all-start) | async-done | bytes 589856 | tf_op jit(solution)/shard_map/all_to_all | solution.py:34
  66.3 2.4 %reshape.149 = bf16[64,2,2,18,2,32]{5,4,3,2,1,0:T(2,128)(2,1)} reshape(bf16[64,2,2304]{2,1,0:T(2,128)(2,1)S(1)} %all-to-all-done) | data formatting | bytes 1179648
  68.6 10.1 %copy.19 = bf16[2,2,32,2,64,18]{5,4,2,3,1,0:T(8,128)(2,1)} copy(bf16[2,2,32,2,64,18]{2,3,5,1,0,4:T(2,128)(2,1)} %bitcast.58) | data formatting | bytes 1179648 | tf_op jit(solution)/shard_map/all_to_all | solution.py:34
  78.7 7.0 %all_to_all.9 = bf16[2,2,32,2,1,1152]{5,2,3,1,0,4:T(8,128)(2,1)S(1)} reshape(bf16[2,2,32,2,64,18]{5,4,2,3,1,0:T(8,128)(2,1)} %copy.19) | data formatting | bytes 1179648 | tf_op jit(solution)/shard_map/all_to_all | solution.py:34
  85.7 0.9 fusion
  86.6 1.6 fusion.13
  88.2 2.2 %copy.20 = bf16[1024,2,2,32]{3,2,1,0:T(2,128)(2,1)S(1)} copy(bf16[1024,2,2,32]{0,3,2,1:T(8,128)(2,1)} %fusion.13) | data formatting | bytes 524288 | tf_op jit(solution)/shard_map/convert_element_type | solution.py:24
  90.4 8.5 %gather_fusion.1 = bf16[1024,2,2,32]{3,2,1,0:T(2,128)(2,1)} fusion(bf16[1024,2,2,32]{3,2,1,0:T(2,128)(2,1)S(1)} %copy.20, s32[1024]{0:T(1024)S(1)} %fusion.33), kind=kCustom, calls=%fused_computation.1 | custom fusion | bytes 528384 | tf_op jit(solution)/shard_map/jit(_take)/gather | solution.py:36
  98.9 5.3 %fusion.34 = bf16[1024,1,2,2,32]{4,3,2,1,0:T(2,128)(2,1)S(1)} fusion(bf16[1024,2,2,32]{3,2,1,0:T(2,128)(2,1)} %gather_fusion.1, pred[1024]{0:T(1024)(128)(4,1)S(1)} %compare_and_fusion), kind=kLoop, calls=%fused_computation.41 | loop fusion | flops 131072 | bytes 525312
  104.3 1.7 reshape.150
  106.0 18.9 %all_to_all.24 = bf16[64,2,1024]{2,1,0:T(2,128)(2,1)} all-to-all(bf16[64,2,1024]{2,1,0:T(2,128)(2,1)} %reshape.150), channel_id=1, replica_groups=mesh['lat'=64,'rad'=8] {'lat'}, dimensions={0} | all-to-all | bytes 524288 | tf_op jit(solution)/shard_map/all_to_all | solution.py:37
  124.9 3.0 %reshape.151 = bf16[1024,1,2,2,32]{4,3,2,1,0:T(2,128)(2,1)S(1)} reshape(bf16[64,2,1024]{2,1,0:T(2,128)(2,1)} %all_to_all.24) | data formatting | bytes 524288
  128.0 2.2 %copy.23 = bf16[64,16,2,2,32]{0,4,2,3,1:T(8,128)(2,1)} copy(bf16[64,16,2,2,32]{4,3,2,1,0:T(2,128)(2,1)S(1)} %bitcast.60) | data formatting | bytes 524288 | tf_op jit(solution)/shard_map/all_to_all | solution.py:37
  130.1 0.0 all-gather.2.cloned.1.call-update
  130.2 1.3 reshape.96
  131.5 51.1 %all-gather.2.cloned.1.call-done = bf16[64,16,2,2,256]{0,4,2,3,1:T(8,128)(2,1)} async-done(((bf16[64,16,2,2,32]{0,4,2,3,1:T(8,128)(2,1)}), bf16[64,16,2,2,256]{0,4,2,3,1:T(8,128)(2,1)}) %all-gather.2.cloned.1.call-update) | async-done | bytes 2097168 | tf_op jit(solution)/shard_map/all_gather | solution.py:45
  182.6 4.4 %convolution_bitcast_fusion = f32[16,64,2,64]{1,3,2,0:T(8,128)} fusion(bf16[64,16,2,2,256]{0,4,2,3,1:T(8,128)(2,1)} %all-gather.2.cloned.1.call-done, bf16[16,64,2,256,1]{3,2,1,0,4:T(2,128)(2,1)S(1)} %bitcast.61), kind=kOutput, calls=%fused_computation.8 | convolution fusion | flops 134217728 | bytes 3670016 | tf_op jit(solution)/shard_map/tqfk,mtfck->tqcm/dot_general | solution.py:42
  187.1 2.2 %copy.25 = f32[16,64,2,64]{3,2,1,0:T(2,128)} copy(f32[16,64,2,64]{1,3,2,0:T(8,128)} %convolution_bitcast_fusion) | data formatting | bytes 1048576 | tf_op jit(solution)/shard_map/tqfk,mtfck->tqcm/transpose | solution.py:42
  (9 shorter events, 0.0 us)
Async XLA Ops:
  6.5 79.2 %copy-start = (bf16[1,1024,1152]{2,1,0:T(8,128)(2,1)S(1)}, bf16[1,1024,1152]{2,1,0:T(8,128)(2,1)}, u32[]{:S(2)}) copy-start(bf16[1,1024,1152]{2,1,0:T(8,128)(2,1)} %param.7) | copy-start | bytes 7077892
  26.0 21.5 %copy-start.2 = (s32[64]{0:T(128)S(1)}, s32[64]{0:T(128)}, u32[]{:S(2)}) copy-start(s32[64]{0:T(128)} %param.9) | copy-start | bytes 772
  26.0 24.0 %copy-start.3 = (s32[64]{0:T(128)S(1)}, s32[64]{0:T(128)}, u32[]{:S(2)}) copy-start(s32[64]{0:T(128)} %param.11) | copy-start | bytes 772
  26.0 25.3 %copy-start.1 = (s32[1024]{0:T(1024)S(1)}, s32[1024]{0:T(1024)}, u32[]{:S(2)}) copy-start(s32[1024]{0:T(1024)} %param.10) | copy-start | bytes 12292
  32.4 33.8 %all-to-all-start = ((bf16[64,2,2304]{2,1,0:T(2,128)(2,1)}), bf16[64,2,2304]{2,1,0:T(2,128)(2,1)S(1)}, u32[]{:S(2)}, u32[]{:S(2)}) async-start(bf16[64,2,2304]{2,1,0:T(2,128)(2,1)} %reshape.148), calls=%async_computation | async-start | bytes 1179648 | tf_op jit(solution)/shard_map/all_to_all | solution.py:34
  47.3 135.4 %all-gather.2.cloned.1.call-start = ((), (), s32[]{:S(2)}) async-start(), calls=%async_computation.2 | async-start | bytes 4718592 | tf_op jit(solution)/shard_map/all_gather | solution.py:45
Sparse Core Ops, SparseCore 0:
  130.3 52.3 all-gather.1
where the time goes:
time: 197 us; the launch traced here: 196 us
  waiting for transfers between devices  66.1 us (34%)
  local copies, waits for them, and re-layouts  64.1 us (33%)
  blocking collectives  18.9 us (10%)
  between operations  16.1 us (8%)
  starting transfers between devices  15 us (8%)
  other arithmetic  9.07 us (5%)
  matrix products  6.89 us (3%)
    all_gather x1, waiting for transfers between devices, on_device(): lax.all_gather(at_owner, 'rad', axis=4, tiled=True)  51.1 us
    unnamed x13, local copies, waits for them, and re-layouts  20.9 us
    all_to_all x1, blocking collectives, on_device(): lax.all_to_all(by_degree, 'lat', split_axis=1, concat_axis=0, tiled=True)  18.9 us
    all_to_all x2, local copies, waits for them, and re-layouts, on_device(): lax.all_to_all(picked, 'lat', split_axis=4, concat_axis=5, tiled=True)  17.1 us
    all_to_all x1, waiting for transfers between devices, on_device(): lax.all_to_all(picked, 'lat', split_axis=4, concat_axis=5, tiled=True)  14.9 us
    all_to_all x1, starting transfers between devices, on_device(): lax.all_to_all(picked, 'lat', split_axis=4, concat_axis=5, tiled=True)  14.8 us
    gather x1, local copies, waits for them, and re-layouts, on_device(): by_degree = jnp.take(coefficients, degree_of_slot, axis=1)  8.5 us
    unnamed x1, other arithmetic  5.34 us
  transfers between devices with their start and end apart: 2, of which 2 were waited for; matrix products, arithmetic and copies ran while one was open for 1% of the time, Pallas kernels for 0%

commit v1 on v0

--- a/solution.py
+++ b/solution.py
@@ -2,6 +2,11 @@
 import jax.numpy as jnp
 from jax import lax
 from jax.sharding import PartitionSpec as P
+
+
+def swapped_in(block, name, dim):
+    repeated = jnp.stack([block] * lax.axis_size(name))
+    return jnp.concatenate(lax.all_to_all(repeated, name, 0, 0), axis=dim)
 
 
 def analyze(received, legendre, first_live):
@@ -42,7 +47,7 @@
     return jnp.einsum(
         "tqfk,mtfck->tqcm",
         matrices,
-        lax.all_gather(at_owner, "rad", axis=4, tiled=True),
+        swapped_in(at_owner, "rad", 4),
         preferred_element_type=jnp.float32,
     )
 

time: 197 us -> 212 us (1.076)
  local copies, waits for them, and re-layouts: 64.1 us -> 87.5 us
  between operations: 16.1 us -> 2.72 us
  starting transfers between devices: 15 us -> 21.6 us
  matrix products: 6.89 us -> 4.73 us
    all_gather x1 -> x0, waiting for transfers between devices: 51.1 us -> none  [on_device(): lax.all_gather(at_owner, 'rad', axis=4, tiled=True)]
    all_to_all x0 -> x1, waiting for transfers between devices: none -> 50.4 us  [swapped_in(): return jnp.concatenate(lax.all_to_all(repeated, name, 0, 0), axis=dim)]
    unnamed x13 -> x16, local copies, waits for them, and re-layouts: 20.9 us -> 40 us
    all_to_all x0 -> x1, starting transfers between devices: none -> 6.82 us  [swapped_in(): return jnp.concatenate(lax.all_to_all(repeated, name, 0, 0), axis=dim)]
    reshape x0 -> x2, local copies, waits for them, and re-layouts: none -> 4.34 us  [swapped_in(): return jnp.concatenate(lax.all_to_all(repeated, name, 0, 0), axis=dim)]
    dot_general x1, matrix products: 4.41 us -> 2.25 us  [on_device(): jnp.einsum('tqfk,mtfck->tqcm', matrices, swapped_in(at_owner, 'rad', 4),...]
    all_to_all x1 -> x0, local copies, waits for them, and re-layouts: 2.16 us -> none  [on_device(): lax.all_to_all(by_degree, 'lat', split_axis=1, concat_axis=0, tiled=True)]
    another operation x0 -> x1, local copies, waits for them, and re-layouts: none -> 2.16 us  [swapped_in(): repeated = jnp.stack([block] * lax.axis_size(name))]
where the time goes in v1:
time: 212 us; the launch traced here: 210 us
  local copies, waits for them, and re-layouts  87.5 us (41%)
  waiting for transfers between devices  65.5 us (31%)
  starting transfers between devices  21.6 us (10%)
  blocking collectives  18.9 us (9%)
  other arithmetic  9.07 us (4%)
  matrix products  4.73 us (2%)
  between operations  2.72 us (1%)
    all_to_all x1, waiting for transfers between devices, swapped_in(): return jnp.concatenate(lax.all_to_all(repeated, name, 0, 0), axis=dim)  50.4 us
    unnamed x16, local copies, waits for them, and re-layouts  40 us
    all_to_all x1, blocking collectives, on_device(): lax.all_to_all(by_degree, 'lat', split_axis=1, concat_axis=0, tiled=True)  18.9 us
    all_to_all x2, local copies, waits for them, and re-layouts, on_device(): lax.all_to_all(picked, 'lat', split_axis=4, concat_axis=5, tiled=True)  17.1 us
    all_to_all x1, waiting for transfers between devices, on_device(): lax.all_to_all(picked, 'lat', split_axis=4, concat_axis=5, tiled=True)  15.1 us
    all_to_all x1, starting transfers between devices, on_device(): lax.all_to_all(picked, 'lat', split_axis=4, concat_axis=5, tiled=True)  14.8 us
    gather x1, local copies, waits for them, and re-layouts, on_device(): by_degree = jnp.take(coefficients, degree_of_slot, axis=1)  8.5 us
    all_to_all x1, starting transfers between devices, swapped_in(): return jnp.concatenate(lax.all_to_all(repeated, name, 0, 0), axis=dim)  6.82 us
  transfers between devices with their start and end apart: 2, of which 2 were waited for; matrix products, arithmetic and copies ran while one was open for 1% of the time, Pallas kernels for 0%

profile of v1, /device:TPU:1, one launch (start us, length us, event | category | flops | bytes accessed | tf_op | source)
XLA Modules:
  0.0 210.1 jit_solution(12507287496259405362)
XLA Ops:
  0.0 0.8 compare_select_fusion.1
  0.8 0.7 compare_and_fusion.1
  1.5 7.4 %copy.18 = bf16[2,2,32,2,64,18]{2,5,3,1,0,4:T(8,128)(2,1)} copy(bf16[2,2,32,2,64,18]{4,3,5,2,1,0:T(2,128)(2,1)} %param.6) | data formatting | bytes 1179648 | tf_op args[0]
  8.9 4.5 %gather_fusion = bf16[64,2,2,32,2,18]{3,5,4,2,1,0:T(8,128)(2,1)} fusion(bf16[2,2,32,2,64,18]{2,5,3,1,0,4:T(8,128)(2,1)} %copy.18, s32[1024]{0:T(1024)S(1)} %pad_clamp_fusion), kind=kCustom, calls=%fused_computation | custom fusion | bytes 1179904 | tf_op jit(solution)/shard_map/jit(_take)/gather | solution.py:38
  13.4 2.2 %select_bitcast_fusion = bf16[2,2,32,2,64,18]{2,5,3,1,0,4:T(8,128)(2,1)S(1)} fusion(bf16[64,2,2,32,2,18]{3,5,4,2,1,0:T(8,128)(2,1)} %gather_fusion, pred[64]{0:T(512)(128)(4,1)S(1)} %compare_and_fusion.1), kind=kLoop, calls=%fused_computation.2 | loop fusion | flops 294912 | bytes 1179712 | tf_op jit(solution)/shard_map/jit(_take)/select_n | solution.py:38
  15.6 3.8 %copy.43 = bf16[2,2,32,2,64,18]{2,3,5,1,0,4:T(2,128)(2,1)} copy(bf16[2,2,32,2,64,18]{2,5,3,1,0,4:T(8,128)(2,1)S(1)} %select_bitcast_fusion) | data formatting | bytes 1179648 | tf_op jit(solution)/shard_map/jit(_take)/select_n | solution.py:38
  19.5 6.4 %reshape.158 = bf16[64,2,2304]{2,1,0:T(2,128)(2,1)} reshape(bf16[64,2,2,18,2,32]{5,4,3,2,1,0:T(2,128)(2,1)} %bitcast.72) | data formatting | bytes 1179648
  25.9 14.8 %all-to-all-start = ((bf16[64,2,2304]{2,1,0:T(2,128)(2,1)}), bf16[64,2,2304]{2,1,0:T(2,128)(2,1)S(1)}, u32[]{:S(2)}, u32[]{:S(2)}) async-start(bf16[64,2,2304]{2,1,0:T(2,128)(2,1)} %reshape.158), calls=%async_computation | async-start | bytes 1179648 | tf_op jit(solution)/shard_map/all_to_all | solution.py:39
  43.3 0.7 dynamic-slice.2
  44.7 15.1 %all-to-all-done = bf16[64,2,2304]{2,1,0:T(2,128)(2,1)S(1)} async-done(((bf16[64,2,2304]{2,1,0:T(2,128)(2,1)}), bf16[64,2,2304]{2,1,0:T(2,128)(2,1)S(1)}, u32[]{:S(2)}, u32[]{:S(2)}) %all-to-all-start) | async-done | bytes 589856 | tf_op jit(solution)/shard_map/all_to_all | solution.py:39
  59.7 2.4 %reshape.159 = bf16[64,2,2,18,2,32]{5,4,3,2,1,0:T(2,128)(2,1)} reshape(bf16[64,2,2304]{2,1,0:T(2,128)(2,1)S(1)} %all-to-all-done) | data formatting | bytes 1179648
  62.1 10.1 %copy.20 = bf16[2,2,32,2,64,18]{5,4,2,3,1,0:T(8,128)(2,1)} copy(bf16[2,2,32,2,64,18]{2,3,5,1,0,4:T(2,128)(2,1)} %bitcast.71) | data formatting | bytes 1179648 | tf_op jit(solution)/shard_map/all_to_all | solution.py:39
  72.2 7.0 %all_to_all.9 = bf16[2,2,32,2,1,1152]{5,2,3,1,0,4:T(8,128)(2,1)S(1)} reshape(bf16[2,2,32,2,64,18]{5,4,2,3,1,0:T(8,128)(2,1)} %copy.20) | data formatting | bytes 1179648 | tf_op jit(solution)/shard_map/all_to_all | solution.py:39
  79.2 0.9 fusion
  80.1 1.6 fusion.13
  81.7 2.2 %copy.21 = bf16[1024,2,2,32]{3,2,1,0:T(2,128)(2,1)S(1)} copy(bf16[1024,2,2,32]{0,3,2,1:T(8,128)(2,1)} %fusion.13) | data formatting | bytes 524288 | tf_op jit(solution)/shard_map/convert_element_type | solution.py:29
  83.9 8.5 %gather_fusion.1 = bf16[1024,2,2,32]{3,2,1,0:T(2,128)(2,1)} fusion(bf16[1024,2,2,32]{3,2,1,0:T(2,128)(2,1)S(1)} %copy.21, s32[1024]{0:T(1024)S(1)} %fusion.34), kind=kCustom, calls=%fused_computation.1 | custom fusion | bytes 528384 | tf_op jit(solution)/shard_map/jit(_take)/gather | solution.py:41
  92.4 5.3 %fusion.35 = bf16[1024,1,2,2,32]{4,3,2,1,0:T(2,128)(2,1)S(1)} fusion(bf16[1024,2,2,32]{3,2,1,0:T(2,128)(2,1)} %gather_fusion.1, pred[1024]{0:T(1024)(128)(4,1)S(1)} %compare_and_fusion), kind=kLoop, calls=%fused_computation.44 | loop fusion | flops 131072 | bytes 525312
  97.8 1.7 reshape.160
  99.5 18.9 %all_to_all.26 = bf16[64,2,1024]{2,1,0:T(2,128)(2,1)} all-to-all(bf16[64,2,1024]{2,1,0:T(2,128)(2,1)} %reshape.160), channel_id=1, replica_groups=mesh['lat'=64,'rad'=8] {'lat'}, dimensions={0} | all-to-all | bytes 524288 | tf_op jit(solution)/shard_map/all_to_all | solution.py:42
  118.4 3.0 %reshape.161 = bf16[1024,1,2,2,32]{4,3,2,1,0:T(2,128)(2,1)S(1)} reshape(bf16[64,2,1024]{2,1,0:T(2,128)(2,1)} %all_to_all.26) | data formatting | bytes 524288
  121.4 2.2 %copy.24 = bf16[64,16,2,2,32]{0,4,3,2,1:T(8,128)(2,1)} copy(bf16[64,16,2,2,32]{4,3,2,1,0:T(2,128)(2,1)S(1)} %bitcast.73) | data formatting | bytes 524288 | tf_op jit(solution)/shard_map/stack | solution.py:8
  123.6 4.0 %broadcast_bitcast_fusion = bf16[8,16,2,2,32,64]{5,4,3,2,1,0:T(8,128)(2,1)} fusion(bf16[64,16,2,2,32]{0,4,3,2,1:T(8,128)(2,1)} %copy.24), kind=kLoop, calls=%fused_computation.43 | loop fusion | bytes 2359296
  127.6 7.6 %reshape.162 = bf16[8,2,65536]{2,1,0:T(2,128)(2,1)} reshape(bf16[8,16,2,2,32,64]{5,4,3,2,1,0:T(8,128)(2,1)} %broadcast_bitcast_fusion) | data formatting | bytes 4194304
  135.3 6.8 %all-to-all-start.2 = ((bf16[8,2,65536]{2,1,0:T(2,128)(2,1)}), bf16[8,2,65536]{2,1,0:T(2,128)(2,1)}, u32[]{:S(2)}, u32[]{:S(2)}) async-start(bf16[8,2,65536]{2,1,0:T(2,128)(2,1)} %reshape.162), calls=%async_computation.2 | async-start | bytes 4194304 | tf_op jit(solution)/shard_map/all_to_all | solution.py:9
  142.1 1.3 reshape.106
  143.4 50.4 %all-to-all-done.2 = bf16[8,2,65536]{2,1,0:T(2,128)(2,1)} async-done(((bf16[8,2,65536]{2,1,0:T(2,128)(2,1)}), bf16[8,2,65536]{2,1,0:T(2,128)(2,1)}, u32[]{:S(2)}, u32[]{:S(2)}) %all-to-all-start.2) | async-done | bytes 2097184 | tf_op jit(solution)/shard_map/all_to_all | solution.py:9
  193.8 7.4 %reshape.163 = bf16[8,16,2,2,32,64]{5,4,3,2,1,0:T(8,128)(2,1)} reshape(bf16[8,2,65536]{2,1,0:T(2,128)(2,1)} %all-to-all-done.2) | data formatting | bytes 4194304
  201.2 3.2 %bitcast_bitcast_fusion = bf16[64,16,2,2,8,32]{0,5,3,2,1,4:T(8,128)(2,1)S(1)} fusion(bf16[8,16,2,2,32,64]{5,4,3,2,1,0:T(8,128)(2,1)} %reshape.163), kind=kLoop, calls=%fused_computation.41 | loop fusion | bytes 4194304 | tf_op jit(solution)/shard_map/reshape | solution.py:9
  204.5 1.1 copy.25
  205.6 2.2 %convolution_bitcast_fusion = f32[16,64,2,64]{1,3,2,0:T(8,128)} fusion(bf16[64,16,2,2,256]{0,4,3,2,1:T(8,128)(2,1)S(1)} %bitcast.70, bf16[16,64,2,256,1]{3,2,1,0,4:T(2,128)(2,1)S(1)} %bitcast.74), kind=kOutput, calls=%fused_computation.8 | convolution fusion | flops 134217728 | bytes 3670016 | tf_op jit(solution)/shard_map/tqfk,mtfck->tqcm/dot_general | solution.py:47
  207.8 2.2 %copy.28 = f32[16,64,2,64]{3,2,1,0:T(2,128)} copy(f32[16,64,2,64]{1,3,2,0:T(8,128)} %convolution_bitcast_fusion) | data formatting | bytes 1048576 | tf_op jit(solution)/shard_map/tqfk,mtfck->tqcm/transpose | solution.py:47
  (13 shorter events, 0.7 us)
Async XLA Ops:
  0.0 79.2 %copy-start = (bf16[1,1024,1152]{2,1,0:T(8,128)(2,1)S(1)}, bf16[1,1024,1152]{2,1,0:T(8,128)(2,1)}, u32[]{:S(2)}) copy-start(bf16[1,1024,1152]{2,1,0:T(8,128)(2,1)} %param.7) | copy-start | bytes 7077892
  19.5 21.3 %copy-start.2 = (s32[64]{0:T(128)S(1)}, s32[64]{0:T(128)}, u32[]{:S(2)}) copy-start(s32[64]{0:T(128)} %param.9) | copy-start | bytes 772
  19.5 23.8 %copy-start.3 = (s32[64]{0:T(128)S(1)}, s32[64]{0:T(128)}, u32[]{:S(2)}) copy-start(s32[64]{0:T(128)} %param.11) | copy-start | bytes 772
  19.5 25.2 %copy-start.1 = (s32[1024]{0:T(1024)S(1)}, s32[1024]{0:T(1024)}, u32[]{:S(2)}) copy-start(s32[1024]{0:T(1024)} %param.10) | copy-start | bytes 12292
  25.9 33.8 %all-to-all-start = ((bf16[64,2,2304]{2,1,0:T(2,128)(2,1)}), bf16[64,2,2304]{2,1,0:T(2,128)(2,1)S(1)}, u32[]{:S(2)}, u32[]{:S(2)}) async-start(bf16[64,2,2304]{2,1,0:T(2,128)(2,1)} %reshape.158), calls=%async_computation | async-start | bytes 1179648 | tf_op jit(solution)/shard_map/all_to_all | solution.py:39
  135.3 58.6 %all-to-all-start.2 = ((bf16[8,2,65536]{2,1,0:T(2,128)(2,1)}), bf16[8,2,65536]{2,1,0:T(2,128)(2,1)}, u32[]{:S(2)}, u32[]{:S(2)}) async-start(bf16[8,2,65536]{2,1,0:T(2,128)(2,1)} %reshape.162), calls=%async_computation.2 | async-start | bytes 4194304 | tf_op jit(solution)/shard_map/all_to_all | solution.py:9
